TPU v7x, 32 devices: a whole 2x2x4 slice. The times are simulated.
32 devices in a mesh: league: 4 (over x, core), env: 8 (over z, y).
Axes of the slice: x: 2, y: 2, z: 4, core: 2. Of those that a mesh axis runs over, the one named last changes fastest.
Arguments:
- obs_own: bfloat16 [4, 2, 128, 16, 2048], P('league', None, 'env'), may hold values from -6 to 6
- obs_opp: bfloat16 [4, 2, 128, 16, 2048], P('league', None, 'env'), may hold values from -6 to 6
- actions: int32 [4, 2, 2, 128, 16], P('league', None, None, 'env'), may hold values from 0 to 255
- opponent_picks: int32 [4, 2], P('league'), may hold values from 0 to 3
- policy_weight: bfloat16 [4, 2048, 2048], P('league', 'env'), may hold values from -0.125 to 0.125
- policy_gain: bfloat16 [4, 2048], P('league'), may hold values from 0.25 to 1.75
- action_table: bfloat16 [256, 2048], replicated, may hold values from -6 to 6
- value_gain: bfloat16 [2048], replicated, may hold values from 0.25 to 1.75
- value_up: bfloat16 [2048, 1024], replicated, may hold values from -0.125 to 0.125
- value_out: bfloat16 [1024], replicated, may hold values from -0.1875 to 0.1875
Outputs:
- learner_rows: bfloat16 [4, 2, 16, 2048, 128], P('league', None, None, 'env')
- values: float32 [4, 2, 128, 16], P('league', None, 'env')
All inputs are finite; a program needn't handle non-finite values.
Results may differ from a plain program's by a relative error of at most 0.0054.
Values may be sent and summed in bfloat16 or wider, within the bound.
A program may use at most 128 MiB of HBM per device.

v0:
```python
import jax
import jax.numpy as jnp
from jax import lax
from jax.sharding import PartitionSpec as P


def rms_norm(inputs, gain):
    scale = lax.rsqrt(jnp.mean(inputs * inputs, axis=-1, keepdims=True) + 1e-05)
    return inputs * scale * gain.astype(jnp.float32)


def local(
    obs_own,
    obs_opp,
    actions,
    opponent_picks,
    policy_weight,
    policy_gain,
    action_table,
    value_gain,
    value_up,
    value_out,
):
    round_count = obs_own.shape[1]
    env_count = obs_own.shape[2]
    step_count = obs_own.shape[3]
    model_width = obs_own.shape[4]
    row_count = env_count * step_count
    weight_shard = policy_weight[0]
    own_gain = policy_gain[0]
    group_count = lax.axis_size("league")
    my_group = lax.axis_index("league")
    own_inputs = obs_own[0].reshape(round_count * row_count, model_width).astype(jnp.float32)
    own_normed = rms_norm(own_inputs, own_gain).astype(jnp.bfloat16)
    own_whole = lax.all_gather(weight_shard, "env", axis=0, tiled=True)
    own_state = own_inputs + jnp.dot(own_normed, own_whole, preferred_element_type=jnp.float32)
    every_pick = lax.all_gather(opponent_picks, "league", axis=0, tiled=True)
    action_range = jnp.arange(action_table.shape[0], dtype=jnp.int32)
    traj_list = []
    value_list = []
    for round_index in range(round_count):
        opp_raw = obs_opp[0, round_index].reshape(row_count, model_width)
        opp_inputs = opp_raw.astype(jnp.float32)
        all_rows = lax.all_gather(opp_raw, "league", axis=0, tiled=True)
        all_normed = rms_norm(all_rows.astype(jnp.float32), own_gain).astype(jnp.bfloat16)
        products = jnp.dot(all_normed, own_whole, preferred_element_type=jnp.float32)
        served = (every_pick[:, round_index] == my_group).astype(jnp.float32)
        products = (
            products.reshape(group_count, row_count, model_width) * served[:, None, None]
        ).reshape(group_count * row_count, model_width)
        opp_state = opp_inputs + lax.psum_scatter(
            products, "league", scatter_dimension=0, tiled=True
        )
        own_ids = actions[0, 0, round_index].reshape(row_count)
        opp_ids = actions[0, 1, round_index].reshape(row_count)
        onehot = (own_ids[:, None] == action_range[None, :]).astype(jnp.bfloat16) + (
            opp_ids[:, None] == action_range[None, :]
        ).astype(jnp.bfloat16)
        action_sum = jnp.dot(onehot, action_table, preferred_element_type=jnp.float32)
        round_state = lax.dynamic_slice_in_dim(own_state, round_index * row_count, row_count, 0)
        joint_sum = round_state + opp_state + action_sum
        joint_row = rms_norm(joint_sum, value_gain).astype(jnp.bfloat16)
        value_hidden = jax.nn.silu(
            jnp.dot(joint_row, value_up, preferred_element_type=jnp.float32)
        ).astype(jnp.bfloat16)
        value_est = jnp.dot(value_hidden, value_out, preferred_element_type=jnp.float32)
        value_list.append(value_est.reshape(env_count, step_count))
        time_block = joint_row.reshape(env_count, step_count, model_width).transpose(1, 2, 0)
        traj_list.append(lax.all_to_all(time_block, "env", split_axis=1, concat_axis=2, tiled=True))
    learner_rows = jnp.stack(traj_list)
    values = jnp.stack(value_list)
    return (learner_rows[None], values[None])


def solution(mesh):
    in_specs = (
        P("league", None, "env", None, None),
        P("league", None, "env", None, None),
        P("league", None, None, "env", None),
        P("league", None),
        P("league", "env", None),
        P("league", None),
        P(),
        P(),
        P(),
        P(),
    )
    out_specs = (P("league", None, None, "env", None), P("league", None, "env", None))
    return jax.shard_map(local, mesh=mesh, in_specs=in_specs, out_specs=out_specs, check_vma=False)
```

profile of v0, /device:TPU:0, one launch (start us, length us, event | category | flops | bytes accessed | tf_op | source)
XLA Modules:
  0.0 480.6 jit_solution(18280044370628031255)
XLA Ops:
  12.0 6.0 %all-gather.1 = s32[4,1,2]{2,1,0:T(1,128)S(1)} all-gather(s32[1,1,2]{2,1,0:T(1,128)S(1)} %bitcast.98), channel_id=1, replica_groups=mesh['league'=4,'env'=8] {'league'}, dimensions={0}, use_global_device_ids=true | all-gather | bytes 40 | tf_op jit(solution)/shard_map/all_gather | solution.py:37
  18.2 29.6 %all-gather.6.cloned.1.call-done = bf16[1024,2048]{1,0:T(8,128)(2,1)} async-done(((bf16[256,2048]{1,0:T(8,128)(2,1)}), bf16[1024,2048]{1,0:T(8,128)(2,1)}) %all-gather.6.cloned.1.call-update) | async-done | bytes 4194320 | tf_op jit(solution)/shard_map/all_gather | solution.py:44
  50.9 124.0 %all-gather.10.cloned.1.call-done = bf16[1,2048,2048]{2,1,0:T(8,128)(2,1)} async-done(((bf16[1,256,2048]{2,1,0:T(8,128)(2,1)}), bf16[1,2048,2048]{2,1,0:T(8,128)(2,1)}) %all-gather.10.cloned.1.call-update) | async-done | bytes 8388624 | tf_op jit(solution)/shard_map/all_gather | solution.py:35
  174.9 14.5 %fusion.12 = f32[1024,2048]{1,0:T(8,128)} fusion(bf16[1,2048,2048]{2,1,0:T(8,128)(2,1)} %all-gather.10.cloned.1.call-done, bf16[1024,2048]{1,0:T(8,128)(2,1)} %all-gather.6.cloned.1.call-done, f32[1024]{0:T(1024)S(1)} %bitcast.94, f32[2048]{0:T(1024)S(1)} %bitcast.90, f32[1024]{0:T(1024)S(1)} %add_rsqrt_fusion.2), kind=kOutput, calls=%fused_computation.16 | convolution fusion | flops 8600420352 | bytes 20987904 | tf_op jit(solution)/shard_map/dot_general | solution.py:46
  189.7 19.5 %all-gather.8.cloned.1.call-done = bf16[1024,2048]{1,0:T(8,128)(2,1)} async-done(((bf16[256,2048]{1,0:T(8,128)(2,1)}), bf16[1024,2048]{1,0:T(8,128)(2,1)}) %all-gather.8.cloned.1.call-update) | async-done | bytes 4194320 | tf_op jit(solution)/shard_map/all_gather | solution.py:44
  212.6 13.6 %fusion.15 = f32[1024,2048]{1,0:T(8,128)} fusion(bf16[1,2048,2048]{2,1,0:T(8,128)(2,1)} %all-gather.10.cloned.1.call-done, bf16[1024,2048]{1,0:T(8,128)(2,1)S(1)} %copy-done.6, f32[1024]{0:T(1024)S(1)} %bitcast.95, f32[1024]{0:T(1024)S(1)} %add_rsqrt_fusion.1, f32[2048]{0:T(1024)S(1)} %bitcast.91), kind=kOutput, calls=%fused_computation.17 | convolution fusion | flops 8600420352 | bytes 20987904 | tf_op jit(solution)/shard_map/dot_general | solution.py:46
  230.2 9.6 %bitcast_add_fusion = f32[512,2048]{1,0:T(8,128)} fusion(bf16[1,2,16,16,2048]{4,3,2,1,0:T(8,128)(2,1)S(1)} %copy-done.5, bf16[512,2048]{1,0:T(8,128)(2,1)S(1)} %fusion.22, bf16[1,2048,2048]{2,1,0:T(8,128)(2,1)} %all-gather.10.cloned.1.call-done), kind=kOutput, calls=%fused_computation.18 | convolution fusion | flops 4297064448 | bytes 16777216 | tf_op jit(solution)/shard_map/dot_general | solution.py:36
  239.9 43.5 %reduce-scatter.3.cloned.1.call-done = f32[256,2048]{1,0:T(8,128)} async-done(((f32[1024,2048]{1,0:T(8,128)}), f32[256,2048]{1,0:T(8,128)}) %reduce-scatter.3.cloned.1.call-update) | async-done | bytes 2097168 | tf_op jit(solution)/shard_map/reduce_scatter | solution.py:51
  283.4 4.2 multiply_reduce_fusion.1
  287.6 70.1 %reduce-scatter.5.cloned.1.call-done = f32[256,2048]{1,0:T(8,128)} async-done(((f32[1024,2048]{1,0:T(8,128)}), f32[256,2048]{1,0:T(8,128)}) %reduce-scatter.5.cloned.1.call-update) | async-done | bytes 2097168 | tf_op jit(solution)/shard_map/reduce_scatter | solution.py:51
  361.3 8.8 %copy.27 = bf16[16,16,2048]{0,1,2:T(8,128)(2,1)} copy(bf16[16,16,2048]{2,1,0:T(8,128)(2,1)S(1)} %bitcast.87) | data formatting | bytes 2097152 | tf_op jit(solution)/shard_map/reshape | solution.py:68
  370.1 7.5 %bitcast_bitcast_fusion = bf16[2048,16,16]{2,1,0:T(8,128)(2,1)} fusion(bf16[16,16,2048]{0,1,2:T(8,128)(2,1)} %copy.27), kind=kLoop, calls=%fused_computation.71 | loop fusion | bytes 2097152
  377.6 11.2 %reshape.107 = bf16[8,2,32768]{2,1,0:T(2,128)(2,1)} reshape(bf16[2048,16,16]{2,1,0:T(8,128)(2,1)} %bitcast_bitcast_fusion) | data formatting | bytes 2097152
  388.8 5.5 %all-to-all-start.1 = ((bf16[8,2,32768]{2,1,0:T(2,128)(2,1)}), bf16[8,2,32768]{2,1,0:T(2,128)(2,1)S(1)}, u32[]{:S(2)}, u32[]{:S(2)}) async-start(bf16[8,2,32768]{2,1,0:T(2,128)(2,1)} %reshape.107), calls=%async_computation.3 | async-start | bytes 2097152 | tf_op jit(solution)/shard_map/all_to_all | solution.py:69
  394.3 8.8 %copy.24 = bf16[16,16,2048]{0,1,2:T(8,128)(2,1)} copy(bf16[16,16,2048]{2,1,0:T(8,128)(2,1)S(1)} %bitcast.86) | data formatting | bytes 2097152 | tf_op jit(solution)/shard_map/reshape | solution.py:68
  403.1 7.5 %bitcast_bitcast_fusion.1 = bf16[2048,16,16]{2,1,0:T(8,128)(2,1)} fusion(bf16[16,16,2048]{0,1,2:T(8,128)(2,1)} %copy.24), kind=kLoop, calls=%fused_computation.72 | loop fusion | bytes 2097152
  410.6 11.2 %reshape.109 = bf16[8,2,32768]{2,1,0:T(2,128)(2,1)} reshape(bf16[2048,16,16]{2,1,0:T(8,128)(2,1)} %bitcast_bitcast_fusion.1) | data formatting | bytes 2097152
  421.8 6.0 %all-to-all-start = ((bf16[8,2,32768]{2,1,0:T(2,128)(2,1)}), bf16[8,2,32768]{2,1,0:T(2,128)(2,1)S(1)}, u32[]{:S(2)}, u32[]{:S(2)}) async-start(bf16[8,2,32768]{2,1,0:T(2,128)(2,1)} %reshape.109), calls=%async_computation.1 | async-start | bytes 2097152 | tf_op jit(solution)/shard_map/all_to_all | solution.py:69
  427.9 3.9 fusion.30
  431.9 4.0 fusion.29
  436.6 7.5 %reshape.108 = bf16[2048,16,16]{2,1,0:T(8,128)(2,1)} reshape(bf16[8,2,32768]{2,1,0:T(2,128)(2,1)S(1)} %all-to-all-done.1) | data formatting | bytes 2097152
  444.1 9.1 %copy.29 = bf16[16,256,8,16]{1,3,2,0:T(8,128)(2,1)} copy(bf16[16,256,8,16]{3,0,1,2:T(8,128)(2,1)} %bitcast.80) | data formatting | bytes 2097152 | tf_op jit(solution)/shard_map/all_to_all | solution.py:69
  453.3 7.5 %reshape.110 = bf16[2048,16,16]{2,1,0:T(8,128)(2,1)} reshape(bf16[8,2,32768]{2,1,0:T(2,128)(2,1)S(1)} %all-to-all-done) | data formatting | bytes 2097152
  460.8 9.1 %copy.26 = bf16[16,256,8,16]{1,3,2,0:T(8,128)(2,1)} copy(bf16[16,256,8,16]{3,0,1,2:T(8,128)(2,1)} %bitcast.81) | data formatting | bytes 2097152 | tf_op jit(solution)/shard_map/all_to_all | solution.py:69
  (71 shorter events, 24.3 us)
Async XLA Ops:
  7.2 276.2 %copy-start = (bf16[256,2048]{1,0:T(8,128)(2,1)S(1)}, bf16[256,2048]{1,0:T(8,128)(2,1)}, u32[]{:S(2)}) copy-start(bf16[256,2048]{1,0:T(8,128)(2,1)} %param.16) | copy-start | bytes 3145732
  7.2 4.8 %copy-start.13 = (s32[1,2]{1,0:T(1,128)S(1)}, s32[1,2]{1,0:T(1,128)}, u32[]{:S(2)}) copy-start(s32[1,2]{1,0:T(1,128)} %param.13) | copy-start | bytes 28
  7.2 11.0 %copy-start.10 = (bf16[1,2048]{1,0:T(2,128)(2,1)S(1)}, bf16[1,2048]{1,0:T(2,128)(2,1)}, u32[]{:S(2)}) copy-start(bf16[1,2048]{1,0:T(2,128)(2,1)} %param.15) | copy-start | bytes 12292
  7.2 40.6 %all-gather.6.cloned.1.call-start = ((), (), s32[]{:S(2)}) async-start(), calls=%async_computation.4 | async-start | bytes 5242880 | tf_op jit(solution)/shard_map/all_gather | solution.py:44
  10.5 164.4 %all-gather.10.cloned.1.call-start = ((), (), s32[]{:S(2)}) async-start(), calls=%async_computation.8 | async-start | bytes 9437184 | tf_op jit(solution)/shard_map/all_gather | solution.py:35
  11.2 197.9 %all-gather.8.cloned.1.call-start = ((), (), s32[]{:S(2)}) async-start(), calls=%async_computation.6 | async-start | bytes 5242880 | tf_op jit(solution)/shard_map/all_gather | solution.py:44
  12.0 271.4 %reduce-scatter.3.cloned.1.call-start = ((), (), s32[]{:S(2)}) async-start(), calls=%async_computation.5 | async-start | bytes 10485760 | tf_op jit(solution)/shard_map/reduce_scatter | solution.py:51
  189.5 168.2 %reduce-scatter.5.cloned.1.call-start = ((), (), s32[]{:S(2)}) async-start(), calls=%async_computation.7 | async-start | bytes 10485760 | tf_op jit(solution)/shard_map/reduce_scatter | solution.py:51
  209.2 3.4 copy-start.6
  226.2 0.8 copy-start.9
  226.2 1.7 copy-start.4
  226.2 2.3 copy-start.11
  228.6 1.6 copy-start.5
  230.2 53.1 %copy-start.2 = (bf16[1,1,16,16,2048]{4,3,2,1,0:T(8,128)(2,1)S(1)}, bf16[1,1,16,16,2048]{4,3,2,1,0:T(8,128)(2,1)}, u32[]{:S(2)}) copy-start(bf16[1,1,16,16,2048]{4,3,2,1,0:T(8,128)(2,1)} %get-tuple-element.8) | copy-start | bytes 3145732
  239.9 117.8 %copy-start.1 = (bf16[1,1,16,16,2048]{4,3,2,1,0:T(8,128)(2,1)S(1)}, bf16[1,1,16,16,2048]{4,3,2,1,0:T(8,128)(2,1)}, u32[]{:S(2)}) copy-start(bf16[1,1,16,16,2048]{4,3,2,1,0:T(8,128)(2,1)} %get-tuple-element.9) | copy-start | bytes 3145732
  357.7 3.1 copy-start.3
  361.2 8.8 %copy-start.8 = (bf16[256,2048]{1,0:T(8,128)(2,1)}, bf16[256,2048]{1,0:T(8,128)(2,1)S(1)}, u32[]{:S(2)}) copy-start(bf16[256,2048]{1,0:T(8,128)(2,1)S(1)} %get-tuple-element.15) | copy-start | bytes 3145732
  361.3 33.1 %copy-start.7 = (bf16[256,2048]{1,0:T(8,128)(2,1)}, bf16[256,2048]{1,0:T(8,128)(2,1)S(1)}, u32[]{:S(2)}) copy-start(bf16[256,2048]{1,0:T(8,128)(2,1)S(1)} %get-tuple-element.14) | copy-start | bytes 3145732
  388.8 33.0 %all-to-all-start.1 = ((bf16[8,2,32768]{2,1,0:T(2,128)(2,1)}), bf16[8,2,32768]{2,1,0:T(2,128)(2,1)S(1)}, u32[]{:S(2)}, u32[]{:S(2)}) async-start(bf16[8,2,32768]{2,1,0:T(2,128)(2,1)} %reshape.107), calls=%async_computation.3 | async-start | bytes 2097152 | tf_op jit(solution)/shard_map/all_to_all | solution.py:69
  410.6 17.2 %copy-start.12 = (bf16[1024]{0:T(1024)(128)(2,1)S(1)}, bf16[1024]{0:T(1024)(128)(2,1)}, u32[]{:S(2)}) copy-start(bf16[1024]{0:T(1024)(128)(2,1)} %param.19) | copy-start | bytes 6148
  421.8 31.4 %all-to-all-start = ((bf16[8,2,32768]{2,1,0:T(2,128)(2,1)}), bf16[8,2,32768]{2,1,0:T(2,128)(2,1)S(1)}, u32[]{:S(2)}, u32[]{:S(2)}) async-start(bf16[8,2,32768]{2,1,0:T(2,128)(2,1)} %reshape.109), calls=%async_computation.1 | async-start | bytes 2097152 | tf_op jit(solution)/shard_map/all_to_all | solution.py:69
Sparse Core Ops, SparseCore 0:
  10.6 37.1 all-gather.5
  49.9 124.9 all-gather.9
  176.5 32.6 all-gather.7
  211.6 71.7 reduce-scatter.2
  286.0 71.6 reduce-scatter.4
where the time goes:
time: 482 us; the launch traced here: 481 us
  waiting for transfers between devices  288 us (60%)
  local copies, waits for them, and re-layouts  97.5 us (20%)
  matrix products  52.9 us (11%)
  between operations  13.9 us (3%)
  starting transfers between devices  11.9 us (2%)
  other arithmetic  10.2 us (2%)
  blocking collectives  5.95 us (1%)
    all_gather x1, waiting for transfers between devices, local(): own_whole = lax.all_gather(weight_shard, 'env', axis=0, tiled=True)  124 us
    reduce_scatter x2, waiting for transfers between devices, local(): lax.psum_scatter(products, 'league', scatter_dimension=0, tiled=True)  114 us
    unnamed x39, local copies, waits for them, and re-layouts  57.8 us
    all_gather x2, waiting for transfers between devices, local(): all_rows = lax.all_gather(opp_raw, 'league', axis=0, tiled=True)  49.1 us
    dot_general x2, matrix products, local(): jnp.dot(all_normed, own_whole, preferred_element_type=jnp.float32)  28.1 us
    all_to_all x2, local copies, waits for them, and re-layouts, local(): lax.all_to_all(time_block, 'env', split_axis=1, concat_axis=2, tiled=True)  18.2 us
    reshape x2, local copies, waits for them, and re-layouts, local(): joint_row.reshape(env_count, step_count, model_width).transpose(1, 2, 0)  17.6 us
    all_to_all x2, starting transfers between devices, local(): lax.all_to_all(time_block, 'env', split_axis=1, concat_axis=2, tiled=True)  11.5 us
  transfers between devices with their start and end apart: 7, of which 5 were waited for; matrix products, arithmetic and copies ran while one was open for 21% of the time, Pallas kernels for 0%

commit v1 on v0

--- a/solution.py
+++ b/solution.py
@@ -41,7 +41,21 @@
     for round_index in range(round_count):
         opp_raw = obs_opp[0, round_index].reshape(row_count, model_width)
         opp_inputs = opp_raw.astype(jnp.float32)
-        all_rows = lax.all_gather(opp_raw, "league", axis=0, tiled=True)
+
+        def store_the_shifts_all(dim_no, page):
+            comm_axis = "league"
+            lanes = jax.lax.axis_size(comm_axis)
+            opened = sorted(((j, (j + 1) % lanes) for j in range(lanes)))
+            u_next = page
+            kept_rows = [u_next]
+            for k in range(1, lanes):
+                u_next = jax.lax.ppermute(u_next, comm_axis, opened)
+                kept_rows.insert(0, u_next)
+            top = jnp.concatenate(kept_rows, axis=dim_no)
+            val = jax.lax.axis_index(comm_axis)
+            return jnp.roll(top, (val + 1) * page.shape[dim_no], axis=dim_no)
+
+        all_rows = store_the_shifts_all(0, opp_raw)
         all_normed = rms_norm(all_rows.astype(jnp.float32), own_gain).astype(jnp.bfloat16)
         products = jnp.dot(all_normed, own_whole, preferred_element_type=jnp.float32)
         served = (every_pick[:, round_index] == my_group).astype(jnp.float32)

time: 482 us -> 421 us (0.87)
  waiting for transfers between devices: 288 us -> 195 us
  blocking collectives: 5.95 us -> 23.2 us
  other arithmetic: 10.2 us -> 24.5 us
    all_gather x1, waiting for transfers between devices: 124 us -> 38.8 us  [local(): own_whole = lax.all_gather(weight_shard, 'env', axis=0, tiled=True)]
    all_gather x2 -> x0, waiting for transfers between devices: 49.1 us -> none  [local(): all_rows = lax.all_gather(opp_raw, 'league', axis=0, tiled=True)]
    ppermute x0 -> x6, waiting for transfers between devices: none -> 45.6 us  [store_the_shifts_all(): u_next = jax.lax.ppermute(u_next, comm_axis, opened)]
    all_gather x1, blocking collectives: 5.95 us -> 23.2 us  [local(): every_pick = lax.all_gather(opponent_picks, 'league', axis=0, tiled=True)]
    reduce_sum x3 -> x2, other arithmetic: 6.75 us -> 19.3 us  [rms_norm(): scale = lax.rsqrt(jnp.mean(inputs * inputs, axis=-1, keepdims=True) + 1e-05)]
    unnamed x39 -> x35, local copies, waits for them, and re-layouts: 57.8 us -> 55.8 us
  transfers between devices with their start and end apart: 7 -> 11, of which waited for: 5 -> 7; matrix products, arithmetic and copies ran while one was open for 21% -> 25% of each run, Pallas kernels for 0% -> 0%
where the time goes in v1:
time: 421 us; the launch traced here: 420 us
  waiting for transfers between devices  195 us (46%)
  local copies, waits for them, and re-layouts  94 us (22%)
  matrix products  54.8 us (13%)
  other arithmetic  24.5 us (6%)
  blocking collectives  23.2 us (6%)
  starting transfers between devices  14.9 us (4%)
  between operations  13.9 us (3%)
    reduce_scatter x2, waiting for transfers between devices, local(): lax.psum_scatter(products, 'league', scatter_dimension=0, tiled=True)  110 us
    unnamed x35, local copies, waits for them, and re-layouts  55.8 us
    ppermute x6, waiting for transfers between devices, store_the_shifts_all(): u_next = jax.lax.ppermute(u_next, comm_axis, opened)  45.6 us
    all_gather x1, waiting for transfers between devices, local(): own_whole = lax.all_gather(weight_shard, 'env', axis=0, tiled=True)  38.8 us
    dot_general x2, matrix products, local(): jnp.dot(all_normed, own_whole, preferred_element_type=jnp.float32)  29.4 us
    all_gather x1, blocking collectives, local(): every_pick = lax.all_gather(opponent_picks, 'league', axis=0, tiled=True)  23.2 us
    reduce_sum x2, other arithmetic, rms_norm(): scale = lax.rsqrt(jnp.mean(inputs * inputs, axis=-1, keepdims=True) + 1e-05)  19.3 us
    all_to_all x2, local copies, waits for them, and re-layouts, local(): lax.all_to_all(time_block, 'env', split_axis=1, concat_axis=2, tiled=True)  18.2 us
  transfers between devices with their start and end apart: 11, of which 7 were waited for; matrix products, arithmetic and copies ran while one was open for 25% of the time, Pallas kernels for 0%

profile of v1, /device:TPU:0, one launch (start us, length us, event | category | flops | bytes accessed | tf_op | source)
XLA Modules:
  0.0 420.0 jit_solution(4237781082797897207)
XLA Ops:
  12.8 11.8 %collective-permute-done = bf16[256,2048]{1,0:T(8,128)(2,1)S(1)} collective-permute-done((bf16[256,2048]{1,0:T(8,128)(2,1)S(1)}, bf16[256,2048]{1,0:T(8,128)(2,1)S(1)}, u32[]{:S(2)}, u32[]{:S(2)}) %collective-permute-start) | collective-permute-done | bytes 1048608 | tf_op jit(solution)/shard_map/ppermute | solution.py:52
  24.6 11.2 %collective-permute-done.3 = bf16[256,2048]{1,0:T(8,128)(2,1)S(1)} collective-permute-done((bf16[256,2048]{1,0:T(8,128)(2,1)S(1)}, bf16[256,2048]{1,0:T(8,128)(2,1)S(1)}, u32[]{:S(2)}, u32[]{:S(2)}) %collective-permute-start.3) | collective-permute-done | bytes 1048608 | tf_op jit(solution)/shard_map/ppermute | solution.py:52
  35.8 11.3 %collective-permute-done.1 = bf16[256,2048]{1,0:T(8,128)(2,1)} collective-permute-done((bf16[256,2048]{1,0:T(8,128)(2,1)S(1)}, bf16[256,2048]{1,0:T(8,128)(2,1)}, u32[]{:S(2)}, u32[]{:S(2)}) %collective-permute-start.1) | collective-permute-done | bytes 1048608 | tf_op jit(solution)/shard_map/ppermute | solution.py:52
  47.2 11.2 %collective-permute-done.4 = bf16[256,2048]{1,0:T(8,128)(2,1)} collective-permute-done((bf16[256,2048]{1,0:T(8,128)(2,1)S(1)}, bf16[256,2048]{1,0:T(8,128)(2,1)}, u32[]{:S(2)}, u32[]{:S(2)}) %collective-permute-start.4) | collective-permute-done | bytes 1048608 | tf_op jit(solution)/shard_map/ppermute | solution.py:52
  58.4 23.2 %all-gather.1 = s32[4,1,2]{2,1,0:T(1,128)S(1)} all-gather(s32[1,1,2]{2,1,0:T(1,128)S(1)} %bitcast.100), channel_id=1, replica_groups=mesh['league'=4,'env'=8] {'league'}, dimensions={0}, use_global_device_ids=true | all-gather | bytes 40 | tf_op jit(solution)/shard_map/all_gather | solution.py:37
  81.8 17.3 %fusion = (f32[1024]{0:T(1024)S(1)}, bf16[1024,2048]{1,0:T(8,128)(2,1)}, f32[1024]{0:T(1024)S(1)}, bf16[1024,2048]{1,0:T(8,128)(2,1)}) fusion(s32[]{:T(128)S(6)} %select_n.13, bf16[256,2048]{1,0:T(8,128)(2,1)S(1)} %bitcast.86, bf16[256,2048]{1,0:T(8,128)(2,1)} %copy-done.5, bf16[256,2048]{1,0:T(8,128)(2,1)} %collective-permute-done.1, ...), kind=kLoop, calls=%fused_computation.4 | loop fusion | flops 79689728 | bytes 16785412 | tf_op jit(solution)/shard_map/reduce_sum | solution.py:8
  99.1 38.8 %all-gather.4.cloned.1.call-done = bf16[1,2048,2048]{2,1,0:T(8,128)(2,1)} async-done(((bf16[1,256,2048]{2,1,0:T(8,128)(2,1)}), bf16[1,2048,2048]{2,1,0:T(8,128)(2,1)}) %all-gather.4.cloned.1.call-update) | async-done | bytes 8388624 | tf_op jit(solution)/shard_map/all_gather | solution.py:35
  137.8 14.6 %fusion.12 = f32[1024,2048]{1,0:T(8,128)} fusion(bf16[1,2048,2048]{2,1,0:T(8,128)(2,1)} %all-gather.4.cloned.1.call-done, bf16[1024,2048]{1,0:T(8,128)(2,1)} %get-tuple-element.10, f32[1024]{0:T(1024)S(1)} %bitcast.96, f32[2048]{0:T(1024)S(1)} %bitcast.92, f32[1024]{0:T(1024)S(1)} %add_rsqrt_fusion.2), kind=kOutput, calls=%fused_computation.32 | convolution fusion | flops 8600420352 | bytes 20987904 | tf_op jit(solution)/shard_map/dot_general | solution.py:60
  152.7 14.7 %fusion.15 = f32[1024,2048]{1,0:T(8,128)} fusion(bf16[1,2048,2048]{2,1,0:T(8,128)(2,1)} %all-gather.4.cloned.1.call-done, bf16[1024,2048]{1,0:T(8,128)(2,1)} %get-tuple-element.28, f32[1024]{0:T(1024)S(1)} %bitcast.97, f32[1024]{0:T(1024)S(1)} %add_rsqrt_fusion.1, f32[2048]{0:T(1024)S(1)} %bitcast.93), kind=kOutput, calls=%fused_computation.33 | convolution fusion | flops 8600420352 | bytes 20987904 | tf_op jit(solution)/shard_map/dot_general | solution.py:60
  173.1 10.2 %bitcast_add_fusion = f32[512,2048]{1,0:T(8,128)} fusion(bf16[1,2,16,16,2048]{4,3,2,1,0:T(8,128)(2,1)S(1)} %copy-done.2, bf16[512,2048]{1,0:T(8,128)(2,1)S(1)} %fusion.36, bf16[1,2048,2048]{2,1,0:T(8,128)(2,1)} %all-gather.4.cloned.1.call-done), kind=kOutput, calls=%fused_computation.48 | convolution fusion | flops 4297064448 | bytes 16777216 | tf_op jit(solution)/shard_map/dot_general | solution.py:36
  183.3 39.3 %reduce-scatter.3.cloned.1.call-done = f32[256,2048]{1,0:T(8,128)} async-done(((f32[1024,2048]{1,0:T(8,128)}), f32[256,2048]{1,0:T(8,128)}) %reduce-scatter.3.cloned.1.call-update) | async-done | bytes 2097168 | tf_op jit(solution)/shard_map/reduce_scatter | solution.py:65
  226.7 70.3 %reduce-scatter.5.cloned.1.call-done = f32[256,2048]{1,0:T(8,128)} async-done(((f32[1024,2048]{1,0:T(8,128)}), f32[256,2048]{1,0:T(8,128)}) %reduce-scatter.5.cloned.1.call-update) | async-done | bytes 2097168 | tf_op jit(solution)/shard_map/reduce_scatter | solution.py:65
  300.6 8.8 %copy.27 = bf16[16,16,2048]{0,1,2:T(8,128)(2,1)} copy(bf16[16,16,2048]{2,1,0:T(8,128)(2,1)S(1)} %bitcast.89) | data formatting | bytes 2097152 | tf_op jit(solution)/shard_map/reshape | solution.py:82
  309.5 7.5 %bitcast_bitcast_fusion = bf16[2048,16,16]{2,1,0:T(8,128)(2,1)} fusion(bf16[16,16,2048]{0,1,2:T(8,128)(2,1)} %copy.27), kind=kLoop, calls=%fused_computation.101 | loop fusion | bytes 2097152
  316.9 11.2 %reshape.107 = bf16[8,2,32768]{2,1,0:T(2,128)(2,1)} reshape(bf16[2048,16,16]{2,1,0:T(8,128)(2,1)} %bitcast_bitcast_fusion) | data formatting | bytes 2097152
  328.2 5.5 %all-to-all-start.1 = ((bf16[8,2,32768]{2,1,0:T(2,128)(2,1)}), bf16[8,2,32768]{2,1,0:T(2,128)(2,1)S(1)}, u32[]{:S(2)}, u32[]{:S(2)}) async-start(bf16[8,2,32768]{2,1,0:T(2,128)(2,1)} %reshape.107), calls=%async_computation.3 | async-start | bytes 2097152 | tf_op jit(solution)/shard_map/all_to_all | solution.py:83
  333.7 8.8 %copy.24 = bf16[16,16,2048]{0,1,2:T(8,128)(2,1)} copy(bf16[16,16,2048]{2,1,0:T(8,128)(2,1)S(1)} %bitcast.88) | data formatting | bytes 2097152 | tf_op jit(solution)/shard_map/reshape | solution.py:82
  342.5 7.5 %bitcast_bitcast_fusion.1 = bf16[2048,16,16]{2,1,0:T(8,128)(2,1)} fusion(bf16[16,16,2048]{0,1,2:T(8,128)(2,1)} %copy.24), kind=kLoop, calls=%fused_computation.102 | loop fusion | bytes 2097152
  350.0 11.2 %reshape.109 = bf16[8,2,32768]{2,1,0:T(2,128)(2,1)} reshape(bf16[2048,16,16]{2,1,0:T(8,128)(2,1)} %bitcast_bitcast_fusion.1) | data formatting | bytes 2097152
  361.2 6.0 %all-to-all-start = ((bf16[8,2,32768]{2,1,0:T(2,128)(2,1)}), bf16[8,2,32768]{2,1,0:T(2,128)(2,1)S(1)}, u32[]{:S(2)}, u32[]{:S(2)}) async-start(bf16[8,2,32768]{2,1,0:T(2,128)(2,1)} %reshape.109), calls=%async_computation.1 | async-start | bytes 2097152 | tf_op jit(solution)/shard_map/all_to_all | solution.py:83
  376.0 7.6 %reshape.108 = bf16[2048,16,16]{2,1,0:T(8,128)(2,1)} reshape(bf16[8,2,32768]{2,1,0:T(2,128)(2,1)S(1)} %all-to-all-done.1) | data formatting | bytes 2097152
  383.5 9.1 %copy.29 = bf16[16,256,8,16]{1,3,2,0:T(8,128)(2,1)} copy(bf16[16,256,8,16]{3,0,1,2:T(8,128)(2,1)} %bitcast.80) | data formatting | bytes 2097152 | tf_op jit(solution)/shard_map/all_to_all | solution.py:83
  392.7 7.6 %reshape.110 = bf16[2048,16,16]{2,1,0:T(8,128)(2,1)} reshape(bf16[8,2,32768]{2,1,0:T(2,128)(2,1)S(1)} %all-to-all-done) | data formatting | bytes 2097152
  400.2 9.1 %copy.26 = bf16[16,256,8,16]{1,3,2,0:T(8,128)(2,1)} copy(bf16[16,256,8,16]{3,0,1,2:T(8,128)(2,1)} %bitcast.81) | data formatting | bytes 2097152 | tf_op jit(solution)/shard_map/all_to_all | solution.py:83
  (72 shorter events, 32.2 us)
Async XLA Ops:
  7.2 215.4 %copy-start = (bf16[256,2048]{1,0:T(8,128)(2,1)S(1)}, bf16[256,2048]{1,0:T(8,128)(2,1)}, u32[]{:S(2)}) copy-start(bf16[256,2048]{1,0:T(8,128)(2,1)} %param.18) | copy-start | bytes 3145732
  7.2 51.2 %copy-start.11 = (s32[1,2]{1,0:T(1,128)S(1)}, s32[1,2]{1,0:T(1,128)}, u32[]{:S(2)}) copy-start(s32[1,2]{1,0:T(1,128)} %param.15) | copy-start | bytes 28
  7.2 74.6 %copy-start.8 = (bf16[1,2048]{1,0:T(2,128)(2,1)S(1)}, bf16[1,2048]{1,0:T(2,128)(2,1)}, u32[]{:S(2)}) copy-start(bf16[1,2048]{1,0:T(2,128)(2,1)} %param.17) | copy-start | bytes 12292
  7.2 130.6 %all-gather.4.cloned.1.call-start = ((), (), s32[]{:S(2)}) async-start(), calls=%async_computation.6 | async-start | bytes 9437184 | tf_op jit(solution)/shard_map/all_gather | solution.py:35
  7.9 214.6 %reduce-scatter.3.cloned.1.call-start = ((), (), s32[]{:S(2)}) async-start(), calls=%async_computation.4 | async-start | bytes 10485760 | tf_op jit(solution)/shard_map/reduce_scatter | solution.py:65
  9.7 14.9 %collective-permute-start = (bf16[256,2048]{1,0:T(8,128)(2,1)S(1)}, bf16[256,2048]{1,0:T(8,128)(2,1)S(1)}, u32[]{:S(2)}, u32[]{:S(2)}) collective-permute-start(bf16[256,2048]{1,0:T(8,128)(2,1)S(1)} %bitcast.85), channel_id=1, source_target_pairs={{0,8},{8,16},{16,24},{24,0},{1,9},{9,17},{17,25},{25,1},{2,10},{10... | collective-permute-start | bytes 3145736 | tf_op jit(solution)/shard_map/ppermute | solution.py:52
  10.2 25.6 %collective-permute-start.3 = (bf16[256,2048]{1,0:T(8,128)(2,1)S(1)}, bf16[256,2048]{1,0:T(8,128)(2,1)S(1)}, u32[]{:S(2)}, u32[]{:S(2)}) collective-permute-start(bf16[256,2048]{1,0:T(8,128)(2,1)S(1)} %bitcast.82), channel_id=1, source_target_pairs={{0,8},{8,16},{16,24},{24,0},{1,9},{9,17},{17,25},{25,1},{2,10},{10... | collective-permute-start | bytes 3145736 | tf_op jit(solution)/shard_map/ppermute | solution.py:52
  24.6 11.2 %copy-start.5 = (bf16[256,2048]{1,0:T(8,128)(2,1)}, bf16[256,2048]{1,0:T(8,128)(2,1)S(1)}, u32[]{:S(2)}) copy-start(bf16[256,2048]{1,0:T(8,128)(2,1)S(1)} %collective-permute-done) | copy-start | bytes 3145732
  24.6 22.6 %collective-permute-start.1 = (bf16[256,2048]{1,0:T(8,128)(2,1)S(1)}, bf16[256,2048]{1,0:T(8,128)(2,1)}, u32[]{:S(2)}, u32[]{:S(2)}) collective-permute-start(bf16[256,2048]{1,0:T(8,128)(2,1)S(1)} %collective-permute-done), channel_id=1, source_target_pairs={{0,8},{8,16},{16,24},{24,0},{1,9},{9,17},{17,25},{25,1},{2,10},{10... | collective-permute-start | bytes 3145736 | tf_op jit(solution)/shard_map/ppermute | solution.py:52
  35.8 11.3 %copy-start.6 = (bf16[256,2048]{1,0:T(8,128)(2,1)}, bf16[256,2048]{1,0:T(8,128)(2,1)S(1)}, u32[]{:S(2)}) copy-start(bf16[256,2048]{1,0:T(8,128)(2,1)S(1)} %collective-permute-done.3) | copy-start | bytes 3145732
  35.8 22.6 %collective-permute-start.4 = (bf16[256,2048]{1,0:T(8,128)(2,1)S(1)}, bf16[256,2048]{1,0:T(8,128)(2,1)}, u32[]{:S(2)}, u32[]{:S(2)}) collective-permute-start(bf16[256,2048]{1,0:T(8,128)(2,1)S(1)} %collective-permute-done.3), channel_id=1, source_target_pairs={{0,8},{8,16},{16,24},{24,0},{1,9},{9,17},{17,25},{25,1},{2,10},{10... | collective-permute-start | bytes 3145736 | tf_op jit(solution)/shard_map/ppermute | solution.py:52
  47.2 34.6 %collective-permute-start.2 = (bf16[256,2048]{1,0:T(8,128)(2,1)}, bf16[256,2048]{1,0:T(8,128)(2,1)}, u32[]{:S(2)}, u32[]{:S(2)}) collective-permute-start(bf16[256,2048]{1,0:T(8,128)(2,1)} %collective-permute-done.1), channel_id=1, source_target_pairs={{0,8},{8,16},{16,24},{24,0},{1,9},{9,17},{17,25},{25,1},{2,10},{10... | collective-permute-start | bytes 3145736 | tf_op jit(solution)/shard_map/ppermute | solution.py:52
  58.4 23.4 %collective-permute-start.5 = (bf16[256,2048]{1,0:T(8,128)(2,1)}, bf16[256,2048]{1,0:T(8,128)(2,1)}, u32[]{:S(2)}, u32[]{:S(2)}) collective-permute-start(bf16[256,2048]{1,0:T(8,128)(2,1)} %collective-permute-done.4), channel_id=1, source_target_pairs={{0,8},{8,16},{16,24},{24,0},{1,9},{9,17},{17,25},{25,1},{2,10},{10... | collective-permute-start | bytes 3145736 | tf_op jit(solution)/shard_map/ppermute | solution.py:52
  152.5 144.6 %reduce-scatter.5.cloned.1.call-start = ((), (), s32[]{:S(2)}) async-start(), calls=%async_computation.5 | async-start | bytes 10485760 | tf_op jit(solution)/shard_map/reduce_scatter | solution.py:65
  167.5 0.8 copy-start.7
  167.5 3.1 copy-start.9
  170.7 2.3 copy-start.2
  297.1 3.1 copy-start.1
  300.6 8.8 %copy-start.4 = (bf16[256,2048]{1,0:T(8,128)(2,1)}, bf16[256,2048]{1,0:T(8,128)(2,1)S(1)}, u32[]{:S(2)}) copy-start(bf16[256,2048]{1,0:T(8,128)(2,1)S(1)} %get-tuple-element.20) | copy-start | bytes 3145732
  300.6 33.1 %copy-start.3 = (bf16[256,2048]{1,0:T(8,128)(2,1)}, bf16[256,2048]{1,0:T(8,128)(2,1)S(1)}, u32[]{:S(2)}) copy-start(bf16[256,2048]{1,0:T(8,128)(2,1)S(1)} %get-tuple-element.19) | copy-start | bytes 3145732
  328.2 33.1 %all-to-all-start.1 = ((bf16[8,2,32768]{2,1,0:T(2,128)(2,1)}), bf16[8,2,32768]{2,1,0:T(2,128)(2,1)S(1)}, u32[]{:S(2)}, u32[]{:S(2)}) async-start(bf16[8,2,32768]{2,1,0:T(2,128)(2,1)} %reshape.107), calls=%async_computation.3 | async-start | bytes 2097152 | tf_op jit(solution)/shard_map/all_to_all | solution.py:83
  350.0 17.2 %copy-start.10 = (bf16[1024]{0:T(1024)(128)(2,1)S(1)}, bf16[1024]{0:T(1024)(128)(2,1)}, u32[]{:S(2)}) copy-start(bf16[1024]{0:T(1024)(128)(2,1)} %param.21) | copy-start | bytes 6148
  361.2 31.4 %all-to-all-start = ((bf16[8,2,32768]{2,1,0:T(2,128)(2,1)}), bf16[8,2,32768]{2,1,0:T(2,128)(2,1)S(1)}, u32[]{:S(2)}, u32[]{:S(2)}) async-start(bf16[8,2,32768]{2,1,0:T(2,128)(2,1)} %reshape.109), calls=%async_computation.1 | async-start | bytes 2097152 | tf_op jit(solution)/shard_map/all_to_all | solution.py:83
Sparse Core Ops, SparseCore 0:
  10.2 127.6 all-gather.3
  152.6 69.8 reduce-scatter.2
  225.3 71.6 reduce-scatter.4
